TPU v7x, 512 devices: a whole 4x4x16 slice. The times are simulated.
512 devices in a mesh: dp: 32 (over y_lo, z), tensor: 16 (over y_hi, x, core).
Axes of the slice: x: 4, y: 4 (y_hi: 2, y_lo: 2; y = y_hi * 2 + y_lo), z: 16, core: 2. Of those that a mesh axis runs over, the one named last changes fastest.
Arguments:
- inputs: bfloat16 [8192, 6144], P('dp', 'tensor'), may hold values from -250 to 250
- upstream: bfloat16 [8192, 4096], P('dp', 'tensor'), may hold values from -6 to 6
- proj_weight: bfloat16 [6144, 4096], P(None, 'tensor'), may hold values from -0.078125 to 0.078125
- proj_bias: float32 [4096], P('tensor'), may hold values from -4 to 4
- norm_gain: float32 [6144], replicated, may hold values from 0.1 to 1.9
- home_rows: int32 [8192], P('dp'), may hold values from 0 to 8191, as said below
Outputs:
- home_grad: bfloat16 [8192, 6144], P('dp', 'tensor')
Inputs may be any that keep to these rules, and one draw needn't show every extreme that they name: `home_rows`: A permutation of 0 to 8191. The balanced row at position i * 256 + k goes to a home row j * 256 + s (0 <= s < 256); of the 256 rows of one dp index, at most 16 have the same owner j, and in every draw some do.
All inputs are finite; a program needn't handle non-finite values.
Results may differ from a plain program's by a relative error of at most 0.018.
Values may be sent and summed in bfloat16 or wider, within the bound.
No kernel may reach another device: no remote copies, remote signals or barrier semaphores. Data moves between devices by JAX's collectives and lax.ppermute only.
A program may use at most 64 MiB of HBM per device.

v0:
```python
import jax
import jax.numpy as jnp
from jax import lax
from jax.experimental import pallas as pl
from jax.experimental.pallas import tpu as pltpu
from jax.sharding import PartitionSpec as P


epsilon = 1e-05
f32, bf16 = jnp.float32, jnp.bfloat16
PAD = 8
CAPACITY = 16
NT = (((1,), (1,)), ((), ()))


def in_vmem(n):
    return [pl.BlockSpec(memory_space=pltpu.VMEM) for _ in range(n)]


def held(*arrays):
    return [pltpu.with_memory_space_constraint(a, pltpu.VMEM) for a in arrays]


def far(*arrays):
    return [pltpu.with_memory_space_constraint(a, pltpu.HBM) for a in arrays]


PARAMS = pltpu.CompilerParams(vmem_limit_bytes=16 * 1024 * 1024)


ANYWHERE = pl.BlockSpec(memory_space=pl.ANY)
SCALAR = pl.BlockSpec(memory_space=pltpu.SMEM)


def spread_kernel(x_any, o_any, x_ref, in_sem, out_sem):
    blocks, rows, _ = o_any.shape
    parts = in_sem.shape[0]
    step = rows // parts
    loads, stores = [], []
    for p in range(parts):
        span = pl.ds(p * step, step)
        loads.append(pltpu.make_async_copy(x_any.at[span], x_ref.at[span], in_sem.at[p]))
        stores.append(
            [
                pltpu.make_async_copy(x_ref.at[span], o_any.at[b, span], out_sem.at[p, b])
                for b in range(blocks)
            ]
        )
    for copy in loads:
        copy.start()
    for p in range(parts):
        loads[p].wait()
        for copy in stores[p]:
            copy.start()
    for part in stores:
        for copy in part:
            copy.wait()


def spread(x, blocks):
    return pl.pallas_call(
        spread_kernel,
        in_specs=[ANYWHERE],
        out_specs=ANYWHERE,
        out_shape=pltpu.HBM((blocks,) + x.shape, x.dtype),
        scratch_shapes=[
            pltpu.VMEM(x.shape, x.dtype),
            pltpu.SemaphoreType.DMA((2,)),
            pltpu.SemaphoreType.DMA((2, blocks)),
        ],
        compiler_params=PARAMS,
        name="spread",
    )(pltpu.with_memory_space_constraint(x, pltpu.HBM))


def prepare_kernel(core_ref, w_any, gain_ref, bias_ref, cut_any, vec_ref, w_ref, w_sem, cut_sem):
    blocks, _, feats, width = w_ref.shape
    core = core_ref[0]
    loads = [pltpu.make_async_copy(w_any.at[b], w_ref.at[b], w_sem.at[b]) for b in range(blocks)]
    stores = [
        pltpu.make_async_copy(w_ref.at[b, 1 - core], cut_any.at[b], cut_sem.at[b]) for b in range(blocks)
    ]
    for copy in loads:
        copy.start()
    row = lax.broadcasted_iota(jnp.int32, (8, feats), 0)
    totals = [jnp.zeros((8, width), f32), jnp.zeros((8, width), f32)]
    for b in range(blocks):
        loads[b].wait()
        stores[b].start()
        for c in range(2):
            gain = jnp.broadcast_to(gain_ref[b, c], (8, feats))
            high = gain.astype(bf16).astype(f32)
            middle = (gain - high).astype(bf16).astype(f32)
            low = gain - high - middle
            pieces = jnp.where(row == 0, high, jnp.where(row == 1, middle, jnp.where(row == 2, low, 0.0)))
            totals[c] += jnp.dot(pieces.astype(bf16), w_ref[b, c], preferred_element_type=f32)
    line = lax.broadcasted_iota(jnp.int32, (8, width), 0)
    even = jnp.sum(totals[0], axis=0, keepdims=True)
    odd = jnp.sum(totals[1], axis=0, keepdims=True)
    vec_ref[...] = jnp.where(line == 0, bias_ref[...], jnp.where(line == 1, even, odd))
    for copy in stores:
        copy.wait()


def prepare(core, weight, gain, bias):
    blocks, _, feats, width = weight.shape
    return pl.pallas_call(
        prepare_kernel,
        in_specs=[SCALAR, ANYWHERE] + in_vmem(2),
        out_specs=[ANYWHERE] + in_vmem(1),
        out_shape=[
            pltpu.HBM((blocks, feats, width), weight.dtype),
            jax.ShapeDtypeStruct((8, width), f32),
        ],
        scratch_shapes=[
            pltpu.VMEM(weight.shape, weight.dtype),
            pltpu.SemaphoreType.DMA((blocks,)),
            pltpu.SemaphoreType.DMA((blocks,)),
        ],
        compiler_params=PARAMS,
        name="prepare",
    )(core, *far(weight), gain, bias)


def weight_copies(core, weight_any, weight_ref, w_sem):
    blocks = weight_ref.shape[0]
    return [
        pltpu.make_async_copy(weight_any.at[b, core], weight_ref.at[b], w_sem.at[b]) for b in range(blocks)
    ]


def forward_kernel(core_ref, x_ref, gain_ref, weight_any, other_ref, q_ref, weight_ref, rows_ref, w_sem):
    blocks, rows, feats = x_ref.shape
    width = weight_ref.shape[2]
    core = core_ref[0]
    w_copies = weight_copies(core, weight_any, weight_ref, w_sem)
    for copy in w_copies:
        copy.start()
    pivot = jnp.mean(x_ref[0].astype(f32), axis=1, keepdims=True)
    total = jnp.zeros((rows, 128), f32)
    square = jnp.zeros((rows, 128), f32)
    for b in range(blocks):
        moved = x_ref[b].astype(f32) - pivot
        for j in range(0, feats, 128):
            part = moved[:, j : j + 128]
            total += part
            square += part * part
        rows_ref[:, b * feats : (b + 1) * feats] = (moved * gain_ref[b, core]).astype(bf16)
        if b % 2 == 1:
            term = jnp.dot(
                rows_ref[:, (b - 1) * feats : (b + 1) * feats],
                other_ref[b - 1 : b + 1].reshape(2 * feats, width),
                preferred_element_type=f32,
            )
            if b == 1:
                q_ref[:, width : 2 * width] = term
            else:
                q_ref[:, width : 2 * width] += term
    shift = jnp.sum(total, axis=1, keepdims=True) / (blocks * feats)
    spread = jnp.sum(square, axis=1, keepdims=True) / (blocks * feats) - shift * shift
    lane = lax.broadcasted_iota(jnp.int32, (rows, 128), 1)
    q_ref[:, 2 * width :] = jnp.where(
        lane == 0, pivot, jnp.where(lane == 1, pivot + shift, jnp.maximum(spread, 0.0))
    )
    for copy in w_copies:
        copy.wait()
    q_ref[:, :width] = jnp.dot(
        rows_ref[...], weight_ref[...].reshape(blocks * feats, width), preferred_element_type=f32
    )


def forward(core, x, gain, weight, other):
    blocks, rows, feats = x.shape
    width = other.shape[2]
    x, other = held(x, other)
    return pl.pallas_call(
        forward_kernel,
        in_specs=[SCALAR] + in_vmem(2) + [ANYWHERE] + in_vmem(1),
        out_specs=in_vmem(1)[0],
        out_shape=jax.ShapeDtypeStruct((rows, 2 * width + 128), f32),
        scratch_shapes=[
            pltpu.VMEM(other.shape, bf16),
            pltpu.VMEM((rows, blocks * feats), bf16),
            pltpu.SemaphoreType.DMA((blocks,)),
        ],
        compiler_params=PARAMS,
        name="forward",
    )(core, x, gain, *far(weight), other)


def backward_kernel(
    core_ref,
    q_ref,
    got_ref,
    up_ref,
    upo_ref,
    vec_ref,
    veco_ref,
    weight_any,
    other_ref,
    p_ref,
    st_ref,
    weight_ref,
    w_sem,
):
    blocks, feats, width = weight_ref.shape
    rows = q_ref.shape[0]
    core = core_ref[0]
    w_copies = weight_copies(core, weight_any, weight_ref, w_sem)
    for copy in w_copies:
        copy.start()
    mine, theirs = q_ref[:, 2 * width :], got_ref[:, 2 * width :]
    gap = 0.5 * (mine[:, 1:2] - theirs[:, 1:2])
    mean = 0.5 * (mine[:, 1:2] + theirs[:, 1:2])
    variance = 0.5 * (mine[:, 2:3] + theirs[:, 2:3]) + gap * gap
    inv_std = lax.rsqrt(variance + epsilon)
    lane = lax.broadcasted_iota(jnp.int32, (rows, 128), 1)
    st_ref[...] = jnp.where(lane == 0, mean, inv_std)
    even = jnp.where(core == 0, mine[:, 0:1], theirs[:, 0:1]) - mean
    odd = jnp.where(core == 0, theirs[:, 0:1], mine[:, 0:1]) - mean

    def grad(summed, up, vec):
        raw = inv_std * (summed + even * vec[1:2, :] + odd * vec[2:3, :])
        preact = raw + vec[0:1, :]
        gate = 1.0 / (1.0 + jnp.exp(-preact))
        pg = (up.astype(f32) * gate * (1.0 + preact * (1.0 - gate))).astype(bf16)
        wide = pg.astype(f32)
        scale = vec[1:2, :] + vec[2:3, :]
        return (
            pg,
            jnp.sum(wide * scale, axis=1, keepdims=True),
            jnp.sum(wide * raw, axis=1, keepdims=True),
        )

    pg, sum_g, sum_gu = grad(q_ref[:, :width] + got_ref[:, width : 2 * width], up_ref[...], vec_ref[...])
    pgo, sum_go, sum_guo = grad(
        q_ref[:, width : 2 * width] + got_ref[:, :width], upo_ref[...], veco_ref[...]
    )
    value = jnp.where(lane < 2, sum_g + sum_go, sum_gu + sum_guo)
    high = value.astype(bf16).astype(f32)
    tail = jnp.where(lane % 2 == 0, high, value - high).T[:PAD].astype(bf16)
    tail = jnp.concatenate([tail, jnp.zeros((PAD, feats - rows), bf16)], axis=1)
    for b in range(blocks):
        w_copies[b].wait()
        p_ref[b, :rows] = (
            lax.dot_general(pg, weight_ref[b], NT, preferred_element_type=f32)
            + lax.dot_general(pgo, other_ref[b], NT, preferred_element_type=f32)
        ).astype(bf16)
        p_ref[b, rows:] = tail


def backward(core, q, got, up, upo, vec, veco, weight, other):
    blocks, feats, _ = other.shape
    rows = q.shape[0]
    return pl.pallas_call(
        backward_kernel,
        in_specs=[SCALAR] + in_vmem(6) + [ANYWHERE] + in_vmem(1),
        out_specs=in_vmem(2),
        out_shape=[
            pltpu.VMEM((blocks, rows + PAD, feats), bf16),
            pltpu.VMEM((rows, 128), f32),
        ],
        scratch_shapes=[
            pltpu.VMEM(other.shape, bf16),
            pltpu.SemaphoreType.DMA((blocks,)),
        ],
        compiler_params=PARAMS,
        name="backward",
    )(core, q, got, up, upo, vec, veco, *far(weight), *held(other))


def finish_kernel(back_ref, x_ref, st_ref, gain_ref, target_ref, slot_ref, send_ref):
    blocks = back_ref.shape[0]
    rows, feats = x_ref.shape
    owners = send_ref.shape[0]
    total = back_ref[0].astype(f32)
    for b in range(1, blocks):
        total += back_ref[b].astype(f32)
    tail = total[rows : rows + 8, :rows]
    sums = tail.T / (2 * blocks * feats)
    first = sums[:, 0:1] + sums[:, 1:2]
    second = sums[:, 2:3] + sums[:, 3:4]
    mean, inv_std = st_ref[:, 0:1], st_ref[:, 1:2]
    unit = (x_ref[...].astype(f32) - mean) * inv_std
    grad = (inv_std * (total[:rows] * gain_ref[...] - first - unit * second)).astype(bf16)
    slots = owners * CAPACITY
    placing = lax.broadcasted_iota(jnp.int32, (slots, rows), 0) == target_ref[...]
    placed = jnp.dot(
        jnp.where(placing, 1.0, 0.0).astype(bf16), grad, preferred_element_type=f32
    ).astype(bf16)
    placed = placed.reshape(owners, CAPACITY, feats)
    for k in range(feats // 128):
        send_ref[:, k * CAPACITY : (k + 1) * CAPACITY, :] = placed[:, :, k * 128 : (k + 1) * 128]
    send_ref[:, feats // 128 * CAPACITY :, :] = jnp.broadcast_to(
        slot_ref[...][:, None, :], (owners, 2, 128)
    )


def finish(back, x, st, gain, target, slot):
    owners = slot.shape[0]
    return pl.pallas_call(
        finish_kernel,
        in_specs=in_vmem(6),
        out_specs=in_vmem(1)[0],
        out_shape=pltpu.VMEM((owners, x.shape[1] // 128 * CAPACITY + 2, 128), bf16),
        compiler_params=PARAMS,
        name="finish",
    )(*held(back, x, st, gain, target, slot))


def landing_kernel(got_ref, o_ref):
    rows, feats = o_ref.shape
    owners = got_ref.shape[0]
    slots = owners * CAPACITY
    pieces = feats // 128
    held_slots = got_ref[:, pieces * CAPACITY, :].astype(bf16)
    spread = lax.broadcasted_iota(jnp.int32, (128, slots), 0) == (
        lax.broadcasted_iota(jnp.int32, (128, slots), 1) % CAPACITY
    )
    every = jnp.dot(held_slots, jnp.where(spread, 1.0, 0.0).astype(bf16), preferred_element_type=f32)
    own = lax.broadcasted_iota(jnp.int32, (owners, slots), 0) == (
        lax.broadcasted_iota(jnp.int32, (owners, slots), 1) // CAPACITY
    )
    slot = jnp.sum(jnp.where(own, every, 0.0), axis=0, keepdims=True).astype(jnp.int32)
    landing = lax.broadcasted_iota(jnp.int32, (rows, slots), 0) == slot
    landing = jnp.where(landing, 1.0, 0.0).astype(bf16)
    for k in range(pieces):
        piece = got_ref[:, k * CAPACITY : (k + 1) * CAPACITY, :].reshape(slots, 128)
        o_ref[:, k * 128 : (k + 1) * 128] = jnp.dot(
            landing, piece, preferred_element_type=f32
        ).astype(bf16)


def land(got, rows, feats):
    return pl.pallas_call(
        landing_kernel,
        in_specs=in_vmem(1),
        out_specs=in_vmem(1)[0],
        out_shape=jax.ShapeDtypeStruct((rows, feats), bf16),
        compiler_params=PARAMS,
        name="land",
    )(*held(got))


def per_device(inputs, upstream, proj_weight, proj_bias, norm_gain, home_rows):
    rows, feats = inputs.shape
    width = upstream.shape[1]
    n_tensor, owners = lax.axis_size("tensor"), lax.axis_size("dp")
    chips = n_tensor // 2
    me = lax.axis_index("tensor")
    core = me % 2
    swap = [(t, t ^ 1) for t in range(n_tensor)]
    classes = [[2 * k + c for k in range(chips)] for c in range(2)]
    core_arr = core.reshape(1).astype(jnp.int32)

    sent = spread(inputs, chips)
    half = lax.all_to_all(sent, "tensor", 0, 0, axis_index_groups=classes, tiled=True)

    pairs = proj_weight.reshape(chips, 2, feats, width)
    gains = norm_gain.reshape(chips, 2, 1, feats)
    cut, vec = prepare(core_arr, pairs, gains, proj_bias[None])
    other = lax.ppermute(cut, "tensor", swap)
    upo = lax.ppermute(upstream, "tensor", swap)
    veco = lax.ppermute(vec, "tensor", swap)

    owner_of = home_rows // rows
    home_slot = home_rows % rows
    order_ids = jnp.arange(rows, dtype=jnp.int32)
    earlier = jnp.sum(
        ((owner_of[:, None] == owner_of[None, :]) & (order_ids[:, None] > order_ids[None, :])).astype(
            jnp.int32
        ),
        axis=1,
    )
    target = owner_of * CAPACITY + earlier
    lanes = jnp.arange(128, dtype=jnp.int32)
    held_at = (jnp.arange(owners, dtype=jnp.int32)[:, None] * CAPACITY + lanes[None, :])[:, :, None]
    match = (held_at == target[None, None, :]) & (lanes < CAPACITY)[None, :, None]
    slot = jnp.sum(jnp.where(match, home_slot[None, None, :] + 1, 0), axis=2) - 1
    slot = slot.astype(f32).astype(bf16)

    own_gain = lax.dynamic_index_in_dim(norm_gain.reshape(n_tensor, 1, feats), me, 0, False)
    half, other, upo, veco, slot, target, own_gain = lax.optimization_barrier(
        (half, other, upo, veco, slot, target, own_gain)
    )
    q = forward(core_arr, half, gains, pairs, other)
    got = lax.ppermute(q, "tensor", swap)
    parts, st = backward(core_arr, q, got, upstream, upo, vec, veco, pairs, other)
    back = lax.all_to_all(parts, "tensor", 0, 0, axis_index_groups=classes, tiled=True)
    send = finish(back, inputs, st, own_gain, target[None, :], slot)
    arrived = lax.all_to_all(send, "dp", split_axis=0, concat_axis=0, tiled=True)
    return land(arrived, rows, feats)


def solution(mesh):
    return jax.shard_map(
        per_device,
        mesh=mesh,
        in_specs=(
            P("dp", "tensor"),
            P("dp", "tensor"),
            P(None, "tensor"),
            P("tensor"),
            P(),
            P("dp"),
        ),
        out_specs=P("dp", "tensor"),
        check_vma=False,
    )
```

profile of v0, /device:TPU:1, one launch (start us, length us, event | category | flops | bytes accessed | tf_op | source)
XLA Modules:
  0.0 123.8 jit_solution(7562436276287724283)
XLA Ops:
  0.0 0.0 copy-start.2
  0.0 0.7 copy-done.2
  0.7 0.0 copy-start.4
  0.7 0.7 copy-done.4
  1.4 2.7 %prepare.1 = (bf16[8,384,256]{2,1,0:T(8,128)(2,1)}, f32[8,256]{1,0:T(8,128)S(1)}) custom-call(s32[1]{0:T(128)} %bitcast.core_ref, bf16[8,2,384,256]{3,2,1,0:T(8,128)(2,1)} %bitcast.13, f32[8,2,1,384]{3,2,1,0:T(1,128)S(1)} %bitcast.8, f32[1,256]{1,0:T(1,128)S(1)} %bitcast.12), custom_call_target="tpu_custom_call" | custom-call | tf_op jit(solution)/shard_map/prepare/pallas_call | solution.py:107
  4.1 0.0 copy-start.1
  4.1 0.0 copy-start.5
  4.1 0.0 copy-start.3
  4.1 8.9 %collective-permute-start = (bf16[8,384,256]{2,1,0:T(8,128)(2,1)}, bf16[8,384,256]{2,1,0:T(8,128)(2,1)S(1)}, u32[]{:S(2)}, u32[]{:S(2)}) collective-permute-start(bf16[8,384,256]{2,1,0:T(8,128)(2,1)} %get-tuple-element.16), channel_id=1, source_target_pairs={{0,1},{1,0},{2,3},{3,2},{4,5},{5,4},{6,7},{7,6},{8,9},{9,8},{10,11... | collective-permute-start | bytes 4718600 | tf_op jit(solution)/shard_map/ppermute | solution.py:362
  13.0 1.9 %collective-permute-start.2 = (f32[8,256]{1,0:T(8,128)S(1)}, f32[8,256]{1,0:T(8,128)S(1)}, u32[]{:S(2)}, u32[]{:S(2)}) collective-permute-start(f32[8,256]{1,0:T(8,128)S(1)} %get-tuple-element.17.vec_ref), channel_id=1, source_target_pairs={{0,1},{1,0},{2,3},{3,2},{4,5},{5,4},{6,7},{7,6},{8,9},{9,8},{10,11... | collective-permute-start | bytes 24584 | tf_op jit(solution)/shard_map/ppermute | solution.py:364
  14.9 2.2 %spread.1 = bf16[8,256,384]{2,1,0:T(8,128)(2,1)} custom-call(bf16[256,384]{1,0:T(8,128)(2,1)} %x_ref.1), custom_call_target="tpu_custom_call" | custom-call | tf_op jit(solution)/shard_map/spread/pallas_call | solution.py:61
  17.2 3.6 %all-to-all-start = ((bf16[8,256,384]{2,1,0:T(8,128)(2,1)}), bf16[8,256,384]{2,1,0:T(8,128)(2,1)S(1)}, u32[]{:S(2)}, u32[]{:S(2)}) async-start(bf16[8,256,384]{2,1,0:T(8,128)(2,1)} %spread.1), calls=%async_computation | async-start | bytes 3145728 | tf_op jit(solution)/shard_map/all_to_all | solution.py:357
  20.8 0.0 copy-done.1
  20.8 2.4 %collective-permute-start.1 = (bf16[256,256]{1,0:T(8,128)(2,1)S(1)}, bf16[256,256]{1,0:T(8,128)(2,1)S(1)}, u32[]{:S(2)}, u32[]{:S(2)}) collective-permute-start(bf16[256,256]{1,0:T(8,128)(2,1)S(1)} %copy-done.1), channel_id=1, source_target_pairs={{0,1},{1,0},{2,3},{3,2},{4,5},{5,4},{6,7},{7,6},{8,9},{9,8},{10,11... | collective-permute-start | bytes 393224 | tf_op jit(solution)/shard_map/ppermute | solution.py:363
  23.2 0.0 copy-done.5
  23.2 0.2 convert_reduce_fusion
  23.4 0.1 iota_add_fusion
  23.5 1.5 %select_reduce_fusion = s32[32,128]{1,0:T(8,128)S(1)} fusion(s32[256]{0:T(256)S(1)} %get-tuple-element.28, s32[256]{0:T(256)S(1)} %multiply_add_fusion, s32[32,128]{1,0:T(8,128)S(1)} %iota_add_fusion, pred[128]{0:T(512)(128)(4,1)S(1)} %iota_compare_fusion.1), kind=kLoop, calls=%fused_computation | loop fusion | flops 4190208 | bytes 34944 | tf_op jit(solution)/shard_map/reduce_sum | solution.py:379
  25.0 0.0 copy-done.3
  25.1 0.0 collective-permute-done.2.veco_ref
  25.1 0.0 collective-permute-done.1.upo_ref
  25.1 18.6 %all-to-all-done.x_ref = bf16[8,256,384]{2,1,0:T(8,128)(2,1)S(1)} async-done(((bf16[8,256,384]{2,1,0:T(8,128)(2,1)}), bf16[8,256,384]{2,1,0:T(8,128)(2,1)S(1)}, u32[]{:S(2)}, u32[]{:S(2)}) %all-to-all-start) | async-done | bytes 1572896 | tf_op jit(solution)/shard_map/all_to_all | solution.py:357
  43.7 0.0 collective-permute-done.other_ref
  43.7 3.5 %forward.1.q_ref = f32[256,640]{1,0:T(8,128)S(1)} custom-call(s32[1]{0:T(128)} %bitcast.core_ref, bf16[8,256,384]{2,1,0:T(8,128)(2,1)S(1)} %all-to-all-done.x_ref, f32[8,2,1,384]{3,2,1,0:T(1,128)S(1)} %bitcast.10, bf16[8,2,384,256]{3,2,1,0:T(8,128)(2,1)} %bitcast.14, bf16[8,384,256]{2,1,0:T(8,128)(2,1)S(1)} %collective-permute-done.other_ref), custom_call_target="tpu_custom_call" | custom-call | tf_op jit(solution)/shard_map/forward/pallas_call | solution.py:176
  47.2 2.7 %collective-permute-start.3 = (f32[256,640]{1,0:T(8,128)S(1)}, f32[256,640]{1,0:T(8,128)S(1)}, u32[]{:S(2)}, u32[]{:S(2)}) collective-permute-start(f32[256,640]{1,0:T(8,128)S(1)} %forward.1.q_ref), channel_id=1, source_target_pairs={{0,1},{1,0},{2,3},{3,2},{4,5},{5,4},{6,7},{7,6},{8,9},{9,8},{10,11... | collective-permute-start | bytes 1966088 | tf_op jit(solution)/shard_map/ppermute | solution.py:387
  49.9 1.7 %collective-permute-done.3.got_ref = f32[256,640]{1,0:T(8,128)S(1)} collective-permute-done((f32[256,640]{1,0:T(8,128)S(1)}, f32[256,640]{1,0:T(8,128)S(1)}, u32[]{:S(2)}, u32[]{:S(2)}) %collective-permute-start.3) | collective-permute-done | bytes 655392 | tf_op jit(solution)/shard_map/ppermute | solution.py:387
  51.6 3.8 %backward.1 = (bf16[8,264,384]{2,1,0:T(8,128)(2,1)S(1)}, f32[256,128]{1,0:T(8,128)S(1)}) custom-call(s32[1]{0:T(128)} %bitcast.core_ref, f32[256,640]{1,0:T(8,128)S(1)} %forward.1.q_ref, f32[256,640]{1,0:T(8,128)S(1)} %collective-permute-done.3.got_ref, bf16[256,256]{1,0:T(8,128)(2,1)S(1)} %copy-done.1, bf16[256,256]{1,0:T(8,128)(2,1)S(1)} %collective-permute-done.1.upo_ref, ...), custom_call_target="tpu_custom_call" | custom-call | tf_op jit(solution)/shard_map/backward/pallas_call | solution.py:255
  55.3 0.0 copy-start
  55.4 27.5 %all_to_all.15.back_ref = bf16[8,264,384]{2,1,0:T(8,128)(2,1)S(1)} all-to-all(bf16[8,264,384]{2,1,0:T(8,128)(2,1)S(1)} %get-tuple-element.22), channel_id=1, replica_groups={{0,2,4,6,8,10,12,14},{1,3,5,7,9,11,13,15},{16,18,20,22,24,26,28,30},{17..., dimensions={0} | all-to-all | bytes 3244032 | tf_op jit(solution)/shard_map/all_to_all | solution.py:389
  82.8 0.0 copy-done
  82.8 0.8 finish.1
  83.7 39.0 %all_to_all.16.got_ref = bf16[32,50,128]{2,1,0:T(8,128)(2,1)S(1)} all-to-all(bf16[32,50,128]{2,1,0:T(8,128)(2,1)S(1)} %finish.1), channel_id=1, replica_groups=mesh['dp'=32,'tensor'=16] {'dp'}, dimensions={0} | all-to-all | bytes 819200 | tf_op jit(solution)/shard_map/all_to_all | solution.py:391
  122.7 1.2 land.1
  (6 shorter events, 0.0 us)
Async XLA Ops:
  0.0 0.7 copy-start.2
  0.7 0.7 copy-start.4
  4.1 16.7 %copy-start.1 = (bf16[256,256]{1,0:T(8,128)(2,1)S(1)}, bf16[256,256]{1,0:T(8,128)(2,1)}, u32[]{:S(2)}) copy-start(bf16[256,256]{1,0:T(8,128)(2,1)} %up_ref.1) | copy-start | bytes 393220
  4.1 19.1 %copy-start.5 = (s32[256]{0:T(256)S(1)}, s32[256]{0:T(256)}, u32[]{:S(2)}) copy-start(s32[256]{0:T(256)} %param.11) | copy-start | bytes 3076
  4.1 20.9 %copy-start.3 = (f32[6144]{0:T(1024)S(1)}, f32[6144]{0:T(1024)}, u32[]{:S(2)}) copy-start(f32[6144]{0:T(1024)} %param.10) | copy-start | bytes 73732
  4.1 39.6 %collective-permute-start = (bf16[8,384,256]{2,1,0:T(8,128)(2,1)}, bf16[8,384,256]{2,1,0:T(8,128)(2,1)S(1)}, u32[]{:S(2)}, u32[]{:S(2)}) collective-permute-start(bf16[8,384,256]{2,1,0:T(8,128)(2,1)} %get-tuple-element.16), channel_id=1, source_target_pairs={{0,1},{1,0},{2,3},{3,2},{4,5},{5,4},{6,7},{7,6},{8,9},{9,8},{10,11... | collective-permute-start | bytes 4718600 | tf_op jit(solution)/shard_map/ppermute | solution.py:362
  13.0 12.1 %collective-permute-start.2 = (f32[8,256]{1,0:T(8,128)S(1)}, f32[8,256]{1,0:T(8,128)S(1)}, u32[]{:S(2)}, u32[]{:S(2)}) collective-permute-start(f32[8,256]{1,0:T(8,128)S(1)} %get-tuple-element.17.vec_ref), channel_id=1, source_target_pairs={{0,1},{1,0},{2,3},{3,2},{4,5},{5,4},{6,7},{7,6},{8,9},{9,8},{10,11... | collective-permute-start | bytes 24584 | tf_op jit(solution)/shard_map/ppermute | solution.py:364
  17.2 26.5 %all-to-all-start = ((bf16[8,256,384]{2,1,0:T(8,128)(2,1)}), bf16[8,256,384]{2,1,0:T(8,128)(2,1)S(1)}, u32[]{:S(2)}, u32[]{:S(2)}) async-start(bf16[8,256,384]{2,1,0:T(8,128)(2,1)} %spread.1), calls=%async_computation | async-start | bytes 3145728 | tf_op jit(solution)/shard_map/all_to_all | solution.py:357
  20.8 4.3 %collective-permute-start.1 = (bf16[256,256]{1,0:T(8,128)(2,1)S(1)}, bf16[256,256]{1,0:T(8,128)(2,1)S(1)}, u32[]{:S(2)}, u32[]{:S(2)}) collective-permute-start(bf16[256,256]{1,0:T(8,128)(2,1)S(1)} %copy-done.1), channel_id=1, source_target_pairs={{0,1},{1,0},{2,3},{3,2},{4,5},{5,4},{6,7},{7,6},{8,9},{9,8},{10,11... | collective-permute-start | bytes 393224 | tf_op jit(solution)/shard_map/ppermute | solution.py:363
  47.2 4.4 %collective-permute-start.3 = (f32[256,640]{1,0:T(8,128)S(1)}, f32[256,640]{1,0:T(8,128)S(1)}, u32[]{:S(2)}, u32[]{:S(2)}) collective-permute-start(f32[256,640]{1,0:T(8,128)S(1)} %forward.1.q_ref), channel_id=1, source_target_pairs={{0,1},{1,0},{2,3},{3,2},{4,5},{5,4},{6,7},{7,6},{8,9},{9,8},{10,11... | collective-permute-start | bytes 1966088 | tf_op jit(solution)/shard_map/ppermute | solution.py:387
  55.3 27.5 %copy-start = (bf16[256,384]{1,0:T(8,128)(2,1)S(1)}, bf16[256,384]{1,0:T(8,128)(2,1)}, u32[]{:S(2)}) copy-start(bf16[256,384]{1,0:T(8,128)(2,1)} %x_ref.1) | copy-start | bytes 589828
where the time goes:
time: 126 us; the launch traced here: 124 us
  blocking collectives  66.5 us (53%)
  waiting for transfers between devices  20.3 us (16%)
  starting transfers between devices  19.5 us (15%)
  Pallas kernels  14.1 us (11%)
  other arithmetic  1.79 us (1%)
  local copies, waits for them, and re-layouts  1.45 us (1%)
    all_to_all x1, blocking collectives, per_device(): lax.all_to_all(send, 'dp', split_axis=0, concat_axis=0, tiled=True)  39 us
    all_to_all x1, blocking collectives, per_device(): lax.all_to_all(parts, 'tensor', 0, 0, axis_index_groups=classes, tiled=True)  27.5 us
    all_to_all x1, waiting for transfers between devices, per_device(): lax.all_to_all(sent, 'tensor', 0, 0, axis_index_groups=classes, tiled=True)  18.6 us
    ppermute x1, starting transfers between devices, per_device(): other = lax.ppermute(cut, 'tensor', swap)  8.88 us
    pallas_call x1, Pallas kernels, backward(): pl.pallas_call(backward_kernel, in_specs=[SCALAR] + in_vmem(6) + [ANYWHER...  3.77 us
    all_to_all x1, starting transfers between devices, per_device(): lax.all_to_all(sent, 'tensor', 0, 0, axis_index_groups=classes, tiled=True)  3.59 us
    pallas_call x1, Pallas kernels, forward(): pl.pallas_call(forward_kernel, in_specs=[SCALAR] + in_vmem(2) + [ANYWHERE...  3.47 us
    ppermute x1, starting transfers between devices, per_device(): got = lax.ppermute(q, 'tensor', swap)  2.69 us
  transfers between devices with their start and end apart: 5, of which 2 were waited for; matrix products, arithmetic and copies ran while one was open for 1% of the time, Pallas kernels for 2%

commit v1 on v0

--- a/solution.py
+++ b/solution.py
@@ -65,8 +65,8 @@
         out_shape=pltpu.HBM((blocks,) + x.shape, x.dtype),
         scratch_shapes=[
             pltpu.VMEM(x.shape, x.dtype),
-            pltpu.SemaphoreType.DMA((2,)),
-            pltpu.SemaphoreType.DMA((2, blocks)),
+            pltpu.SemaphoreType.DMA((4,)),
+            pltpu.SemaphoreType.DMA((4, blocks)),
         ],
         compiler_params=PARAMS,
         name="spread",
@@ -146,21 +146,14 @@
             total += part
             square += part * part
         rows_ref[:, b * feats : (b + 1) * feats] = (moved * gain_ref[b, core]).astype(bf16)
-        if b % 2 == 1:
-            term = jnp.dot(
-                rows_ref[:, (b - 1) * feats : (b + 1) * feats],
-                other_ref[b - 1 : b + 1].reshape(2 * feats, width),
-                preferred_element_type=f32,
-            )
-            if b == 1:
-                q_ref[:, width : 2 * width] = term
-            else:
-                q_ref[:, width : 2 * width] += term
     shift = jnp.sum(total, axis=1, keepdims=True) / (blocks * feats)
     spread = jnp.sum(square, axis=1, keepdims=True) / (blocks * feats) - shift * shift
     lane = lax.broadcasted_iota(jnp.int32, (rows, 128), 1)
     q_ref[:, 2 * width :] = jnp.where(
         lane == 0, pivot, jnp.where(lane == 1, pivot + shift, jnp.maximum(spread, 0.0))
+    )
+    q_ref[:, width : 2 * width] = jnp.dot(
+        rows_ref[...], other_ref[...].reshape(blocks * feats, width), preferred_element_type=f32
     )
     for copy in w_copies:
         copy.wait()
@@ -308,7 +301,7 @@
     )(*held(back, x, st, gain, target, slot))
 
 
-def landing_kernel(got_ref, o_ref):
+def landing_kernel(got_ref, o_any, o_ref, sem):
     rows, feats = o_ref.shape
     owners = got_ref.shape[0]
     slots = owners * CAPACITY
@@ -324,19 +317,27 @@
     slot = jnp.sum(jnp.where(own, every, 0.0), axis=0, keepdims=True).astype(jnp.int32)
     landing = lax.broadcasted_iota(jnp.int32, (rows, slots), 0) == slot
     landing = jnp.where(landing, 1.0, 0.0).astype(bf16)
+    copies = []
     for k in range(pieces):
         piece = got_ref[:, k * CAPACITY : (k + 1) * CAPACITY, :].reshape(slots, 128)
-        o_ref[:, k * 128 : (k + 1) * 128] = jnp.dot(
-            landing, piece, preferred_element_type=f32
-        ).astype(bf16)
+        span = pl.ds(k * 128, 128)
+        o_ref[:, span] = jnp.dot(landing, piece, preferred_element_type=f32).astype(bf16)
+        copies.append(pltpu.make_async_copy(o_ref.at[:, span], o_any.at[:, span], sem.at[k]))
+        copies[k].start()
+    for copy in copies:
+        copy.wait()
 
 
 def land(got, rows, feats):
     return pl.pallas_call(
         landing_kernel,
         in_specs=in_vmem(1),
-        out_specs=in_vmem(1)[0],
-        out_shape=jax.ShapeDtypeStruct((rows, feats), bf16),
+        out_specs=ANYWHERE,
+        out_shape=pltpu.HBM((rows, feats), bf16),
+        scratch_shapes=[
+            pltpu.VMEM((rows, feats), bf16),
+            pltpu.SemaphoreType.DMA((feats // 128,)),
+        ],
         compiler_params=PARAMS,
         name="land",
     )(*held(got))

time: 126 us -> 126 us (level)
  no operation moved by 1% of the time
where the time goes in v1:
time: 126 us; the launch traced here: 124 us
  blocking collectives  66.4 us (53%)
  waiting for transfers between devices  20.3 us (16%)
  starting transfers between devices  19.5 us (15%)
  Pallas kernels  14.1 us (11%)
  other arithmetic  1.79 us (1%)
  local copies, waits for them, and re-layouts  1.45 us (1%)
    all_to_all x1, blocking collectives, per_device(): lax.all_to_all(send, 'dp', split_axis=0, concat_axis=0, tiled=True)  38.9 us
    all_to_all x1, blocking collectives, per_device(): lax.all_to_all(parts, 'tensor', 0, 0, axis_index_groups=classes, tiled=True)  27.5 us
    all_to_all x1, waiting for transfers between devices, per_device(): lax.all_to_all(sent, 'tensor', 0, 0, axis_index_groups=classes, tiled=True)  18.6 us
    ppermute x1, starting transfers between devices, per_device(): other = lax.ppermute(cut, 'tensor', swap)  8.88 us
    pallas_call x1, Pallas kernels, backward(): pl.pallas_call(backward_kernel, in_specs=[SCALAR] + in_vmem(6) + [ANYWHER...  3.77 us
    all_to_all x1, starting transfers between devices, per_device(): lax.all_to_all(sent, 'tensor', 0, 0, axis_index_groups=classes, tiled=True)  3.59 us
    pallas_call x1, Pallas kernels, forward(): pl.pallas_call(forward_kernel, in_specs=[SCALAR] + in_vmem(2) + [ANYWHERE...  3.46 us
    ppermute x1, starting transfers between devices, per_device(): got = lax.ppermute(q, 'tensor', swap)  2.69 us
  transfers between devices with their start and end apart: 5, of which 2 were waited for; matrix products, arithmetic and copies ran while one was open for 1% of the time, Pallas kernels for 2%

profile of v1, /device:TPU:1, one launch (start us, length us, event | category | flops | bytes accessed | tf_op | source)
XLA Modules:
  0.0 123.8 jit_solution(13749618263219580904)
XLA Ops:
  0.0 0.0 copy-start.2
  0.0 0.7 copy-done.2
  0.7 0.0 copy-start.4
  0.7 0.7 copy-done.4
  1.4 2.7 %prepare.1 = (bf16[8,384,256]{2,1,0:T(8,128)(2,1)}, f32[8,256]{1,0:T(8,128)S(1)}) custom-call(s32[1]{0:T(128)} %bitcast.core_ref, bf16[8,2,384,256]{3,2,1,0:T(8,128)(2,1)} %bitcast.13, f32[8,2,1,384]{3,2,1,0:T(1,128)S(1)} %bitcast.8, f32[1,256]{1,0:T(1,128)S(1)} %bitcast.12), custom_call_target="tpu_custom_call" | custom-call | tf_op jit(solution)/shard_map/prepare/pallas_call | solution.py:107
  4.1 0.0 copy-start.1
  4.1 0.0 copy-start.5
  4.1 0.0 copy-start.3
  4.1 8.9 %collective-permute-start = (bf16[8,384,256]{2,1,0:T(8,128)(2,1)}, bf16[8,384,256]{2,1,0:T(8,128)(2,1)S(1)}, u32[]{:S(2)}, u32[]{:S(2)}) collective-permute-start(bf16[8,384,256]{2,1,0:T(8,128)(2,1)} %get-tuple-element.16), channel_id=1, source_target_pairs={{0,1},{1,0},{2,3},{3,2},{4,5},{5,4},{6,7},{7,6},{8,9},{9,8},{10,11... | collective-permute-start | bytes 4718600 | tf_op jit(solution)/shard_map/ppermute | solution.py:363
  13.0 1.9 %collective-permute-start.2 = (f32[8,256]{1,0:T(8,128)S(1)}, f32[8,256]{1,0:T(8,128)S(1)}, u32[]{:S(2)}, u32[]{:S(2)}) collective-permute-start(f32[8,256]{1,0:T(8,128)S(1)} %get-tuple-element.17.vec_ref), channel_id=1, source_target_pairs={{0,1},{1,0},{2,3},{3,2},{4,5},{5,4},{6,7},{7,6},{8,9},{9,8},{10,11... | collective-permute-start | bytes 24584 | tf_op jit(solution)/shard_map/ppermute | solution.py:365
  14.9 2.3 %spread.1 = bf16[8,256,384]{2,1,0:T(8,128)(2,1)} custom-call(bf16[256,384]{1,0:T(8,128)(2,1)} %x_ref.1), custom_call_target="tpu_custom_call" | custom-call | tf_op jit(solution)/shard_map/spread/pallas_call | solution.py:61
  17.2 3.6 %all-to-all-start = ((bf16[8,256,384]{2,1,0:T(8,128)(2,1)}), bf16[8,256,384]{2,1,0:T(8,128)(2,1)S(1)}, u32[]{:S(2)}, u32[]{:S(2)}) async-start(bf16[8,256,384]{2,1,0:T(8,128)(2,1)} %spread.1), calls=%async_computation | async-start | bytes 3145728 | tf_op jit(solution)/shard_map/all_to_all | solution.py:358
  20.8 0.0 copy-done.1
  20.8 2.4 %collective-permute-start.1 = (bf16[256,256]{1,0:T(8,128)(2,1)S(1)}, bf16[256,256]{1,0:T(8,128)(2,1)S(1)}, u32[]{:S(2)}, u32[]{:S(2)}) collective-permute-start(bf16[256,256]{1,0:T(8,128)(2,1)S(1)} %copy-done.1), channel_id=1, source_target_pairs={{0,1},{1,0},{2,3},{3,2},{4,5},{5,4},{6,7},{7,6},{8,9},{9,8},{10,11... | collective-permute-start | bytes 393224 | tf_op jit(solution)/shard_map/ppermute | solution.py:364
  23.3 0.0 copy-done.5
  23.3 0.2 convert_reduce_fusion
  23.5 0.1 iota_add_fusion
  23.6 1.5 %select_reduce_fusion = s32[32,128]{1,0:T(8,128)S(1)} fusion(s32[256]{0:T(256)S(1)} %get-tuple-element.28, s32[256]{0:T(256)S(1)} %multiply_add_fusion, s32[32,128]{1,0:T(8,128)S(1)} %iota_add_fusion, pred[128]{0:T(512)(128)(4,1)S(1)} %iota_compare_fusion.1), kind=kLoop, calls=%fused_computation | loop fusion | flops 4190208 | bytes 34944 | tf_op jit(solution)/shard_map/reduce_sum | solution.py:380
  25.1 0.0 copy-done.3
  25.1 0.0 collective-permute-done.2.veco_ref
  25.1 0.0 collective-permute-done.1.upo_ref
  25.1 18.6 %all-to-all-done.x_ref = bf16[8,256,384]{2,1,0:T(8,128)(2,1)S(1)} async-done(((bf16[8,256,384]{2,1,0:T(8,128)(2,1)}), bf16[8,256,384]{2,1,0:T(8,128)(2,1)S(1)}, u32[]{:S(2)}, u32[]{:S(2)}) %all-to-all-start) | async-done | bytes 1572896 | tf_op jit(solution)/shard_map/all_to_all | solution.py:358
  43.7 0.0 collective-permute-done.other_ref
  43.7 3.5 %forward.1.q_ref = f32[256,640]{1,0:T(8,128)S(1)} custom-call(s32[1]{0:T(128)} %bitcast.core_ref, bf16[8,256,384]{2,1,0:T(8,128)(2,1)S(1)} %all-to-all-done.x_ref, f32[8,2,1,384]{3,2,1,0:T(1,128)S(1)} %bitcast.10, bf16[8,2,384,256]{3,2,1,0:T(8,128)(2,1)} %bitcast.14, bf16[8,384,256]{2,1,0:T(8,128)(2,1)S(1)} %collective-permute-done.other_ref), custom_call_target="tpu_custom_call" | custom-call | tf_op jit(solution)/shard_map/forward/pallas_call | solution.py:169
  47.2 2.7 %collective-permute-start.3 = (f32[256,640]{1,0:T(8,128)S(1)}, f32[256,640]{1,0:T(8,128)S(1)}, u32[]{:S(2)}, u32[]{:S(2)}) collective-permute-start(f32[256,640]{1,0:T(8,128)S(1)} %forward.1.q_ref), channel_id=1, source_target_pairs={{0,1},{1,0},{2,3},{3,2},{4,5},{5,4},{6,7},{7,6},{8,9},{9,8},{10,11... | collective-permute-start | bytes 1966088 | tf_op jit(solution)/shard_map/ppermute | solution.py:388
  49.9 1.7 %collective-permute-done.3.got_ref = f32[256,640]{1,0:T(8,128)S(1)} collective-permute-done((f32[256,640]{1,0:T(8,128)S(1)}, f32[256,640]{1,0:T(8,128)S(1)}, u32[]{:S(2)}, u32[]{:S(2)}) %collective-permute-start.3) | collective-permute-done | bytes 655392 | tf_op jit(solution)/shard_map/ppermute | solution.py:388
  51.6 3.8 %backward.1 = (bf16[8,264,384]{2,1,0:T(8,128)(2,1)S(1)}, f32[256,128]{1,0:T(8,128)S(1)}) custom-call(s32[1]{0:T(128)} %bitcast.core_ref, f32[256,640]{1,0:T(8,128)S(1)} %forward.1.q_ref, f32[256,640]{1,0:T(8,128)S(1)} %collective-permute-done.3.got_ref, bf16[256,256]{1,0:T(8,128)(2,1)S(1)} %copy-done.1, bf16[256,256]{1,0:T(8,128)(2,1)S(1)} %collective-permute-done.1.upo_ref, ...), custom_call_target="tpu_custom_call" | custom-call | tf_op jit(solution)/shard_map/backward/pallas_call | solution.py:248
  55.4 0.0 copy-start
  55.4 27.5 %all_to_all.15.back_ref = bf16[8,264,384]{2,1,0:T(8,128)(2,1)S(1)} all-to-all(bf16[8,264,384]{2,1,0:T(8,128)(2,1)S(1)} %get-tuple-element.22), channel_id=1, replica_groups={{0,2,4,6,8,10,12,14},{1,3,5,7,9,11,13,15},{16,18,20,22,24,26,28,30},{17..., dimensions={0} | all-to-all | bytes 3244032 | tf_op jit(solution)/shard_map/all_to_all | solution.py:390
  82.9 0.0 copy-done
  82.9 0.8 finish.1
  83.7 38.9 %all_to_all.16.got_ref = bf16[32,50,128]{2,1,0:T(8,128)(2,1)S(1)} all-to-all(bf16[32,50,128]{2,1,0:T(8,128)(2,1)S(1)} %finish.1), channel_id=1, replica_groups=mesh['dp'=32,'tensor'=16] {'dp'}, dimensions={0} | all-to-all | bytes 819200 | tf_op jit(solution)/shard_map/all_to_all | solution.py:392
  122.7 1.1 land.1
  (6 shorter events, 0.0 us)
Async XLA Ops:
  0.0 0.7 copy-start.2
  0.7 0.7 copy-start.4
  4.1 16.7 %copy-start.1 = (bf16[256,256]{1,0:T(8,128)(2,1)S(1)}, bf16[256,256]{1,0:T(8,128)(2,1)}, u32[]{:S(2)}) copy-start(bf16[256,256]{1,0:T(8,128)(2,1)} %up_ref.1) | copy-start | bytes 393220
  4.1 19.2 %copy-start.5 = (s32[256]{0:T(256)S(1)}, s32[256]{0:T(256)}, u32[]{:S(2)}) copy-start(s32[256]{0:T(256)} %param.11) | copy-start | bytes 3076
  4.1 21.0 %copy-start.3 = (f32[6144]{0:T(1024)S(1)}, f32[6144]{0:T(1024)}, u32[]{:S(2)}) copy-start(f32[6144]{0:T(1024)} %param.10) | copy-start | bytes 73732
  4.1 39.6 %collective-permute-start = (bf16[8,384,256]{2,1,0:T(8,128)(2,1)}, bf16[8,384,256]{2,1,0:T(8,128)(2,1)S(1)}, u32[]{:S(2)}, u32[]{:S(2)}) collective-permute-start(bf16[8,384,256]{2,1,0:T(8,128)(2,1)} %get-tuple-element.16), channel_id=1, source_target_pairs={{0,1},{1,0},{2,3},{3,2},{4,5},{5,4},{6,7},{7,6},{8,9},{9,8},{10,11... | collective-permute-start | bytes 4718600 | tf_op jit(solution)/shard_map/ppermute | solution.py:363
  13.0 12.1 %collective-permute-start.2 = (f32[8,256]{1,0:T(8,128)S(1)}, f32[8,256]{1,0:T(8,128)S(1)}, u32[]{:S(2)}, u32[]{:S(2)}) collective-permute-start(f32[8,256]{1,0:T(8,128)S(1)} %get-tuple-element.17.vec_ref), channel_id=1, source_target_pairs={{0,1},{1,0},{2,3},{3,2},{4,5},{5,4},{6,7},{7,6},{8,9},{9,8},{10,11... | collective-permute-start | bytes 24584 | tf_op jit(solution)/shard_map/ppermute | solution.py:365
  17.2 26.5 %all-to-all-start = ((bf16[8,256,384]{2,1,0:T(8,128)(2,1)}), bf16[8,256,384]{2,1,0:T(8,128)(2,1)S(1)}, u32[]{:S(2)}, u32[]{:S(2)}) async-start(bf16[8,256,384]{2,1,0:T(8,128)(2,1)} %spread.1), calls=%async_computation | async-start | bytes 3145728 | tf_op jit(solution)/shard_map/all_to_all | solution.py:358
  20.8 4.3 %collective-permute-start.1 = (bf16[256,256]{1,0:T(8,128)(2,1)S(1)}, bf16[256,256]{1,0:T(8,128)(2,1)S(1)}, u32[]{:S(2)}, u32[]{:S(2)}) collective-permute-start(bf16[256,256]{1,0:T(8,128)(2,1)S(1)} %copy-done.1), channel_id=1, source_target_pairs={{0,1},{1,0},{2,3},{3,2},{4,5},{5,4},{6,7},{7,6},{8,9},{9,8},{10,11... | collective-permute-start | bytes 393224 | tf_op jit(solution)/shard_map/ppermute | solution.py:364
  47.2 4.4 %collective-permute-start.3 = (f32[256,640]{1,0:T(8,128)S(1)}, f32[256,640]{1,0:T(8,128)S(1)}, u32[]{:S(2)}, u32[]{:S(2)}) collective-permute-start(f32[256,640]{1,0:T(8,128)S(1)} %forward.1.q_ref), channel_id=1, source_target_pairs={{0,1},{1,0},{2,3},{3,2},{4,5},{5,4},{6,7},{7,6},{8,9},{9,8},{10,11... | collective-permute-start | bytes 1966088 | tf_op jit(solution)/shard_map/ppermute | solution.py:388
  55.4 27.5 %copy-start = (bf16[256,384]{1,0:T(8,128)(2,1)S(1)}, bf16[256,384]{1,0:T(8,128)(2,1)}, u32[]{:S(2)}) copy-start(bf16[256,384]{1,0:T(8,128)(2,1)} %x_ref.1) | copy-start | bytes 589828

commit v2 on v0

--- a/solution.py
+++ b/solution.py
@@ -65,8 +65,8 @@
         out_shape=pltpu.HBM((blocks,) + x.shape, x.dtype),
         scratch_shapes=[
             pltpu.VMEM(x.shape, x.dtype),
-            pltpu.SemaphoreType.DMA((2,)),
-            pltpu.SemaphoreType.DMA((2, blocks)),
+            pltpu.SemaphoreType.DMA((1,)),
+            pltpu.SemaphoreType.DMA((1, blocks)),
         ],
         compiler_params=PARAMS,
         name="spread",
@@ -146,21 +146,14 @@
             total += part
             square += part * part
         rows_ref[:, b * feats : (b + 1) * feats] = (moved * gain_ref[b, core]).astype(bf16)
-        if b % 2 == 1:
-            term = jnp.dot(
-                rows_ref[:, (b - 1) * feats : (b + 1) * feats],
-                other_ref[b - 1 : b + 1].reshape(2 * feats, width),
-                preferred_element_type=f32,
-            )
-            if b == 1:
-                q_ref[:, width : 2 * width] = term
-            else:
-                q_ref[:, width : 2 * width] += term
     shift = jnp.sum(total, axis=1, keepdims=True) / (blocks * feats)
     spread = jnp.sum(square, axis=1, keepdims=True) / (blocks * feats) - shift * shift
     lane = lax.broadcasted_iota(jnp.int32, (rows, 128), 1)
     q_ref[:, 2 * width :] = jnp.where(
         lane == 0, pivot, jnp.where(lane == 1, pivot + shift, jnp.maximum(spread, 0.0))
+    )
+    q_ref[:, width : 2 * width] = jnp.dot(
+        rows_ref[...], other_ref[...].reshape(blocks * feats, width), preferred_element_type=f32
     )
     for copy in w_copies:
         copy.wait()

time: 126 us -> 126 us (level)
  no operation moved by 1% of the time
where the time goes in v2:
time: 126 us; the launch traced here: 124 us
  blocking collectives  66.4 us (53%)
  waiting for transfers between devices  20.3 us (16%)
  starting transfers between devices  19.5 us (15%)
  Pallas kernels  14 us (11%)
  other arithmetic  1.79 us (1%)
  local copies, waits for them, and re-layouts  1.45 us (1%)
    all_to_all x1, blocking collectives, per_device(): lax.all_to_all(send, 'dp', split_axis=0, concat_axis=0, tiled=True)  38.9 us
    all_to_all x1, blocking collectives, per_device(): lax.all_to_all(parts, 'tensor', 0, 0, axis_index_groups=classes, tiled=True)  27.5 us
    all_to_all x1, waiting for transfers between devices, per_device(): lax.all_to_all(sent, 'tensor', 0, 0, axis_index_groups=classes, tiled=True)  18.6 us
    ppermute x1, starting transfers between devices, per_device(): other = lax.ppermute(cut, 'tensor', swap)  8.88 us
    pallas_call x1, Pallas kernels, backward(): pl.pallas_call(backward_kernel, in_specs=[SCALAR] + in_vmem(6) + [ANYWHER...  3.77 us
    all_to_all x1, starting transfers between devices, per_device(): lax.all_to_all(sent, 'tensor', 0, 0, axis_index_groups=classes, tiled=True)  3.59 us
    pallas_call x1, Pallas kernels, forward(): pl.pallas_call(forward_kernel, in_specs=[SCALAR] + in_vmem(2) + [ANYWHERE...  3.46 us
    ppermute x1, starting transfers between devices, per_device(): got = lax.ppermute(q, 'tensor', swap)  2.69 us
  transfers between devices with their start and end apart: 5, of which 2 were waited for; matrix products, arithmetic and copies ran while one was open for 1% of the time, Pallas kernels for 2%

profile of v2, /device:TPU:1, one launch (start us, length us, event | category | flops | bytes accessed | tf_op | source)
XLA Modules:
  0.0 123.7 jit_solution(9449745393317846535)
XLA Ops:
  0.0 0.0 copy-start.2
  0.0 0.7 copy-done.2
  0.7 0.0 copy-start.4
  0.7 0.7 copy-done.4
  1.4 2.7 %prepare.1 = (bf16[8,384,256]{2,1,0:T(8,128)(2,1)}, f32[8,256]{1,0:T(8,128)S(1)}) custom-call(s32[1]{0:T(128)} %bitcast.core_ref, bf16[8,2,384,256]{3,2,1,0:T(8,128)(2,1)} %bitcast.13, f32[8,2,1,384]{3,2,1,0:T(1,128)S(1)} %bitcast.8, f32[1,256]{1,0:T(1,128)S(1)} %bitcast.12), custom_call_target="tpu_custom_call" | custom-call | tf_op jit(solution)/shard_map/prepare/pallas_call | solution.py:107
  4.1 0.0 copy-start.1
  4.1 0.0 copy-start.5
  4.1 0.0 copy-start.3
  4.1 8.9 %collective-permute-start = (bf16[8,384,256]{2,1,0:T(8,128)(2,1)}, bf16[8,384,256]{2,1,0:T(8,128)(2,1)S(1)}, u32[]{:S(2)}, u32[]{:S(2)}) collective-permute-start(bf16[8,384,256]{2,1,0:T(8,128)(2,1)} %get-tuple-element.16), channel_id=1, source_target_pairs={{0,1},{1,0},{2,3},{3,2},{4,5},{5,4},{6,7},{7,6},{8,9},{9,8},{10,11... | collective-permute-start | bytes 4718600 | tf_op jit(solution)/shard_map/ppermute | solution.py:355
  13.0 1.9 %collective-permute-start.2 = (f32[8,256]{1,0:T(8,128)S(1)}, f32[8,256]{1,0:T(8,128)S(1)}, u32[]{:S(2)}, u32[]{:S(2)}) collective-permute-start(f32[8,256]{1,0:T(8,128)S(1)} %get-tuple-element.17.vec_ref), channel_id=1, source_target_pairs={{0,1},{1,0},{2,3},{3,2},{4,5},{5,4},{6,7},{7,6},{8,9},{9,8},{10,11... | collective-permute-start | bytes 24584 | tf_op jit(solution)/shard_map/ppermute | solution.py:357
  14.9 2.2 %spread.1 = bf16[8,256,384]{2,1,0:T(8,128)(2,1)} custom-call(bf16[256,384]{1,0:T(8,128)(2,1)} %x_ref.1), custom_call_target="tpu_custom_call" | custom-call | tf_op jit(solution)/shard_map/spread/pallas_call | solution.py:61
  17.1 3.6 %all-to-all-start = ((bf16[8,256,384]{2,1,0:T(8,128)(2,1)}), bf16[8,256,384]{2,1,0:T(8,128)(2,1)S(1)}, u32[]{:S(2)}, u32[]{:S(2)}) async-start(bf16[8,256,384]{2,1,0:T(8,128)(2,1)} %spread.1), calls=%async_computation | async-start | bytes 3145728 | tf_op jit(solution)/shard_map/all_to_all | solution.py:350
  20.7 0.0 copy-done.1
  20.7 2.4 %collective-permute-start.1 = (bf16[256,256]{1,0:T(8,128)(2,1)S(1)}, bf16[256,256]{1,0:T(8,128)(2,1)S(1)}, u32[]{:S(2)}, u32[]{:S(2)}) collective-permute-start(bf16[256,256]{1,0:T(8,128)(2,1)S(1)} %copy-done.1), channel_id=1, source_target_pairs={{0,1},{1,0},{2,3},{3,2},{4,5},{5,4},{6,7},{7,6},{8,9},{9,8},{10,11... | collective-permute-start | bytes 393224 | tf_op jit(solution)/shard_map/ppermute | solution.py:356
  23.1 0.0 copy-done.5
  23.2 0.2 convert_reduce_fusion
  23.4 0.1 iota_add_fusion
  23.4 1.5 %select_reduce_fusion = s32[32,128]{1,0:T(8,128)S(1)} fusion(s32[256]{0:T(256)S(1)} %get-tuple-element.28, s32[256]{0:T(256)S(1)} %multiply_add_fusion, s32[32,128]{1,0:T(8,128)S(1)} %iota_add_fusion, pred[128]{0:T(512)(128)(4,1)S(1)} %iota_compare_fusion.1), kind=kLoop, calls=%fused_computation | loop fusion | flops 4190208 | bytes 34944 | tf_op jit(solution)/shard_map/reduce_sum | solution.py:372
  25.0 0.0 copy-done.3
  25.0 0.0 collective-permute-done.2.veco_ref
  25.0 0.0 collective-permute-done.1.upo_ref
  25.0 18.6 %all-to-all-done.x_ref = bf16[8,256,384]{2,1,0:T(8,128)(2,1)S(1)} async-done(((bf16[8,256,384]{2,1,0:T(8,128)(2,1)}), bf16[8,256,384]{2,1,0:T(8,128)(2,1)S(1)}, u32[]{:S(2)}, u32[]{:S(2)}) %all-to-all-start) | async-done | bytes 1572896 | tf_op jit(solution)/shard_map/all_to_all | solution.py:350
  43.6 0.0 collective-permute-done.other_ref
  43.6 3.5 %forward.1.q_ref = f32[256,640]{1,0:T(8,128)S(1)} custom-call(s32[1]{0:T(128)} %bitcast.core_ref, bf16[8,256,384]{2,1,0:T(8,128)(2,1)S(1)} %all-to-all-done.x_ref, f32[8,2,1,384]{3,2,1,0:T(1,128)S(1)} %bitcast.10, bf16[8,2,384,256]{3,2,1,0:T(8,128)(2,1)} %bitcast.14, bf16[8,384,256]{2,1,0:T(8,128)(2,1)S(1)} %collective-permute-done.other_ref), custom_call_target="tpu_custom_call" | custom-call | tf_op jit(solution)/shard_map/forward/pallas_call | solution.py:169
  47.1 2.7 %collective-permute-start.3 = (f32[256,640]{1,0:T(8,128)S(1)}, f32[256,640]{1,0:T(8,128)S(1)}, u32[]{:S(2)}, u32[]{:S(2)}) collective-permute-start(f32[256,640]{1,0:T(8,128)S(1)} %forward.1.q_ref), channel_id=1, source_target_pairs={{0,1},{1,0},{2,3},{3,2},{4,5},{5,4},{6,7},{7,6},{8,9},{9,8},{10,11... | collective-permute-start | bytes 1966088 | tf_op jit(solution)/shard_map/ppermute | solution.py:380
  49.8 1.7 %collective-permute-done.3.got_ref = f32[256,640]{1,0:T(8,128)S(1)} collective-permute-done((f32[256,640]{1,0:T(8,128)S(1)}, f32[256,640]{1,0:T(8,128)S(1)}, u32[]{:S(2)}, u32[]{:S(2)}) %collective-permute-start.3) | collective-permute-done | bytes 655392 | tf_op jit(solution)/shard_map/ppermute | solution.py:380
  51.5 3.8 %backward.1 = (bf16[8,264,384]{2,1,0:T(8,128)(2,1)S(1)}, f32[256,128]{1,0:T(8,128)S(1)}) custom-call(s32[1]{0:T(128)} %bitcast.core_ref, f32[256,640]{1,0:T(8,128)S(1)} %forward.1.q_ref, f32[256,640]{1,0:T(8,128)S(1)} %collective-permute-done.3.got_ref, bf16[256,256]{1,0:T(8,128)(2,1)S(1)} %copy-done.1, bf16[256,256]{1,0:T(8,128)(2,1)S(1)} %collective-permute-done.1.upo_ref, ...), custom_call_target="tpu_custom_call" | custom-call | tf_op jit(solution)/shard_map/backward/pallas_call | solution.py:248
  55.3 0.0 copy-start
  55.3 27.5 %all_to_all.15.back_ref = bf16[8,264,384]{2,1,0:T(8,128)(2,1)S(1)} all-to-all(bf16[8,264,384]{2,1,0:T(8,128)(2,1)S(1)} %get-tuple-element.22), channel_id=1, replica_groups={{0,2,4,6,8,10,12,14},{1,3,5,7,9,11,13,15},{16,18,20,22,24,26,28,30},{17..., dimensions={0} | all-to-all | bytes 3244032 | tf_op jit(solution)/shard_map/all_to_all | solution.py:382
  82.8 0.0 copy-done
  82.8 0.8 finish.1
  83.6 38.9 %all_to_all.16.got_ref = bf16[32,50,128]{2,1,0:T(8,128)(2,1)S(1)} all-to-all(bf16[32,50,128]{2,1,0:T(8,128)(2,1)S(1)} %finish.1), channel_id=1, replica_groups=mesh['dp'=32,'tensor'=16] {'dp'}, dimensions={0} | all-to-all | bytes 819200 | tf_op jit(solution)/shard_map/all_to_all | solution.py:384
  122.5 1.2 land.1
  (6 shorter events, 0.0 us)
Async XLA Ops:
  0.0 0.7 copy-start.2
  0.7 0.7 copy-start.4
  4.1 16.6 %copy-start.1 = (bf16[256,256]{1,0:T(8,128)(2,1)S(1)}, bf16[256,256]{1,0:T(8,128)(2,1)}, u32[]{:S(2)}) copy-start(bf16[256,256]{1,0:T(8,128)(2,1)} %up_ref.1) | copy-start | bytes 393220
  4.1 19.0 %copy-start.5 = (s32[256]{0:T(256)S(1)}, s32[256]{0:T(256)}, u32[]{:S(2)}) copy-start(s32[256]{0:T(256)} %param.11) | copy-start | bytes 3076
  4.1 20.9 %copy-start.3 = (f32[6144]{0:T(1024)S(1)}, f32[6144]{0:T(1024)}, u32[]{:S(2)}) copy-start(f32[6144]{0:T(1024)} %param.10) | copy-start | bytes 73732
  4.1 39.5 %collective-permute-start = (bf16[8,384,256]{2,1,0:T(8,128)(2,1)}, bf16[8,384,256]{2,1,0:T(8,128)(2,1)S(1)}, u32[]{:S(2)}, u32[]{:S(2)}) collective-permute-start(bf16[8,384,256]{2,1,0:T(8,128)(2,1)} %get-tuple-element.16), channel_id=1, source_target_pairs={{0,1},{1,0},{2,3},{3,2},{4,5},{5,4},{6,7},{7,6},{8,9},{9,8},{10,11... | collective-permute-start | bytes 4718600 | tf_op jit(solution)/shard_map/ppermute | solution.py:355
  13.0 12.0 %collective-permute-start.2 = (f32[8,256]{1,0:T(8,128)S(1)}, f32[8,256]{1,0:T(8,128)S(1)}, u32[]{:S(2)}, u32[]{:S(2)}) collective-permute-start(f32[8,256]{1,0:T(8,128)S(1)} %get-tuple-element.17.vec_ref), channel_id=1, source_target_pairs={{0,1},{1,0},{2,3},{3,2},{4,5},{5,4},{6,7},{7,6},{8,9},{9,8},{10,11... | collective-permute-start | bytes 24584 | tf_op jit(solution)/shard_map/ppermute | solution.py:357
  17.1 26.5 %all-to-all-start = ((bf16[8,256,384]{2,1,0:T(8,128)(2,1)}), bf16[8,256,384]{2,1,0:T(8,128)(2,1)S(1)}, u32[]{:S(2)}, u32[]{:S(2)}) async-start(bf16[8,256,384]{2,1,0:T(8,128)(2,1)} %spread.1), calls=%async_computation | async-start | bytes 3145728 | tf_op jit(solution)/shard_map/all_to_all | solution.py:350
  20.7 4.3 %collective-permute-start.1 = (bf16[256,256]{1,0:T(8,128)(2,1)S(1)}, bf16[256,256]{1,0:T(8,128)(2,1)S(1)}, u32[]{:S(2)}, u32[]{:S(2)}) collective-permute-start(bf16[256,256]{1,0:T(8,128)(2,1)S(1)} %copy-done.1), channel_id=1, source_target_pairs={{0,1},{1,0},{2,3},{3,2},{4,5},{5,4},{6,7},{7,6},{8,9},{9,8},{10,11... | collective-permute-start | bytes 393224 | tf_op jit(solution)/shard_map/ppermute | solution.py:356
  47.1 4.4 %collective-permute-start.3 = (f32[256,640]{1,0:T(8,128)S(1)}, f32[256,640]{1,0:T(8,128)S(1)}, u32[]{:S(2)}, u32[]{:S(2)}) collective-permute-start(f32[256,640]{1,0:T(8,128)S(1)} %forward.1.q_ref), channel_id=1, source_target_pairs={{0,1},{1,0},{2,3},{3,2},{4,5},{5,4},{6,7},{7,6},{8,9},{9,8},{10,11... | collective-permute-start | bytes 1966088 | tf_op jit(solution)/shard_map/ppermute | solution.py:380
  55.3 27.5 %copy-start = (bf16[256,384]{1,0:T(8,128)(2,1)S(1)}, bf16[256,384]{1,0:T(8,128)(2,1)}, u32[]{:S(2)}) copy-start(bf16[256,384]{1,0:T(8,128)(2,1)} %x_ref.1) | copy-start | bytes 589828
